TPU v7x, 32 devices: a whole 2x2x4 slice. The times are simulated.
32 devices in a mesh: section: 4 (over y, core), tp: 8 (over z, x).
Axes of the slice: x: 2, y: 2, z: 4, core: 2. Of those that a mesh axis runs over, the one named last changes fastest.
Arguments:
- section_inputs: bfloat16 [4, 2, 64, 8192], P('section', None, 'tp'), may hold values from -6 to 6
- norm_gain: bfloat16 [4, 8192], P('section'), may hold values from 0.5 to 1.5
- w_query: bfloat16 [4, 8192, 4096], P('section', None, 'tp'), may hold values from -0.0625 to 0.0625
- key_projection: bfloat16 [4, 8192, 512], P('section', 'tp'), may hold values from -0.0625 to 0.0625
- value_projection: bfloat16 [4, 8192, 512], P('section', 'tp'), may hold values from -0.0625 to 0.0625
- w_out: bfloat16 [4, 4096, 8192], P('section', 'tp'), may hold values from -0.09375 to 0.09375
- token_dir: bfloat16 [2, 64, 8192], P(None, 'tp'), may hold values from -6 to 6
- tok_logratio: float32 [2, 64], P(None, 'tp'), may hold values from -4 to 4
- segment_ids: int32 [2, 64], replicated, may hold values from 0 to 7, as said below
- pair_of_slot: int32 [2, 4], replicated, may hold values from 0 to 7, as said below
- pair_counts: int32 [8, 2], replicated, may hold values from 1 to 24, as said below
Outputs:
- input_grads: bfloat16 [4, 2, 64, 8192], P('section', None, 'tp')
- grad_w_query: bfloat16 [4, 8192, 4096], P('section', None, 'tp')
- grad_w_key: bfloat16 [4, 8192, 512], P('section', 'tp')
- grad_w_value: bfloat16 [4, 8192, 512], P('section', 'tp')
- grad_w_out: bfloat16 [4, 4096, 8192], P('section', 'tp')
- grad_norm_gain: float32 [4, 8192], P('section')
Inputs may be any that keep to these rules, and one draw needn't show every extreme that they name: `segment_ids`: in each micro-batch the segment ids do not fall along the tokens and take every value of 0 to 7; segment 2 j is the chosen and 2 j + 1 the rejected sequence of slot j; each sequence has 1 to 24 tokens and one of each micro-batch has exactly 24. `pair_of_slot`: every pair stands in exactly one slot. pair_counts[p] holds the token counts of the chosen and the rejected sequence of pair p as they stand in segment_ids.
All inputs are finite; a program needn't handle non-finite values.
Results may differ from a plain program's by a relative error of at most 0.038.
Values may be sent and summed in bfloat16 or wider, within the bound.
A program may use at most 192 MiB of HBM per device.

v0:
```python
import math

import jax
import jax.numpy as jnp
from jax import lax
from jax.sharding import PartitionSpec as P

HEAD_WIDTH = 128
QUERY_HEAD_COUNT = 32
SLOTS = 4


norm_epsilon = 1e-05
pair_beta = 4.0
masked_score = -1e30


def passed_along(value, axis, steps):
    count = lax.axis_size(axis)
    leading, last = (max(0, -steps), min(count, count - steps))
    return lax.ppermute(value, axis, [(source, source + steps) for source in range(leading, last)])


def pair_weights(seq_sums, pair_of_slot, pair_counts):
    table = (
        pair_of_slot[:, :, None] == jnp.arange(pair_counts.shape[0], dtype=jnp.int32)[None, None, :]
    ).astype(jnp.float32)
    counts = jnp.einsum("msp,pc->msc", table, pair_counts.astype(jnp.float32))
    margin = pair_beta * (seq_sums[:, 0::2] / counts[:, :, 0] - seq_sums[:, 1::2] / counts[:, :, 1])
    weight = pair_beta * jax.nn.sigmoid(-margin)
    stacked = jnp.stack([-weight / counts[:, :, 0], weight / counts[:, :, 1]], -1)
    return stacked.reshape(seq_sums.shape)


def contract_last(left, right):
    return lax.dot_general(
        left, right, (((1,), (1,)), ((), ())), preferred_element_type=jnp.float32
    )


def body(
    section_inputs,
    norm_gain,
    w_query,
    key_projection,
    value_projection,
    w_out,
    token_dir,
    tok_logratio,
    segment_ids,
    pair_of_slot,
    pair_counts,
):
    section_count = lax.axis_size("section")
    tp_count = lax.axis_size("tp")
    section_index = lax.axis_index("section")
    tp_index = lax.axis_index("tp")
    saved = section_inputs[0]
    batch_groups, rows, width = saved.shape
    token_total = rows * tp_count
    gain_values = norm_gain[0].astype(jnp.float32)
    query_weight = w_query[0]
    key_weight = key_projection[0]
    value_weight = value_projection[0]
    out_weight = w_out[0]
    head_cols = query_weight.shape[1]
    local_heads = head_cols // HEAD_WIDTH
    slice_width = key_weight.shape[0]
    key_width = key_weight.shape[1]
    key_count = key_width // HEAD_WIDTH
    query_group = QUERY_HEAD_COUNT // key_count
    seq_count = 2 * SLOTS
    scale = 1.0 / math.sqrt(HEAD_WIDTH)
    own_rows = saved.astype(jnp.float32)
    own_inverse = lax.rsqrt(jnp.mean(own_rows * own_rows, -1, keepdims=True) + norm_epsilon)
    own_unit = own_rows * own_inverse
    whole = lax.all_gather(saved, "tp", axis=1, tiled=True)
    whole_wide = whole.astype(jnp.float32)
    whole_inverse = lax.rsqrt(jnp.mean(whole_wide * whole_wide, -1, keepdims=True) + norm_epsilon)
    normed = (whole_wide * whole_inverse * gain_values).astype(jnp.bfloat16)
    queries = jnp.einsum(
        "mtd,dc->mtc", normed, query_weight, preferred_element_type=jnp.float32
    ).astype(jnp.bfloat16)
    normed_cols = lax.dynamic_slice_in_dim(normed, tp_index * slice_width, slice_width, 2)
    key_part = jnp.einsum(
        "mtd,dc->mtc", normed_cols, key_weight, preferred_element_type=jnp.float32
    )
    value_part = jnp.einsum(
        "mtd,dc->mtc", normed_cols, value_weight, preferred_element_type=jnp.float32
    )
    segment_rows = lax.dynamic_slice_in_dim(segment_ids, tp_index * rows, rows, 1)
    member = (
        segment_rows[:, :, None] == jnp.arange(seq_count, dtype=jnp.int32)[None, None, :]
    ).astype(jnp.float32)
    partial_sums = jnp.einsum("mt,mts->ms", tok_logratio, member)
    key_sum, value_sum, seq_sums = (
        lax.psum(key_part.astype(jnp.bfloat16), "tp").astype(jnp.float32),
        lax.psum(value_part.astype(jnp.bfloat16), "tp").astype(jnp.float32),
        lax.psum(partial_sums.astype(jnp.bfloat16), "tp").astype(jnp.float32),
    )
    key_tensor = key_sum.astype(jnp.bfloat16)
    value_tensor = value_sum.astype(jnp.bfloat16)
    weights = pair_weights(seq_sums, pair_of_slot, pair_counts)
    token_weight = jnp.einsum("mts,ms->mt", member, weights)
    top_rows = (token_weight[:, :, None] * token_dir.astype(jnp.float32)).astype(jnp.bfloat16)
    head_ids = tp_index * local_heads + jnp.arange(local_heads, dtype=jnp.int32)
    key_pick = (head_ids // query_group)[:, None] == jnp.arange(key_count, dtype=jnp.int32)[None, :]
    pick_low = key_pick.astype(jnp.bfloat16)
    pick_wide = key_pick.astype(jnp.float32)
    query_heads = queries.reshape(batch_groups, token_total, local_heads, HEAD_WIDTH)
    heads_of_key = jnp.einsum(
        "mtkc,hk->mthc",
        key_tensor.reshape(batch_groups, token_total, key_count, HEAD_WIDTH),
        pick_low,
        preferred_element_type=jnp.float32,
    ).astype(jnp.bfloat16)
    heads_of_value = jnp.einsum(
        "mtkc,hk->mthc",
        value_tensor.reshape(batch_groups, token_total, key_count, HEAD_WIDTH),
        pick_low,
        preferred_element_type=jnp.float32,
    ).astype(jnp.bfloat16)
    position = jnp.arange(token_total, dtype=jnp.int32)
    allowed = (segment_ids[:, :, None] == segment_ids[:, None, :]) & (
        position[:, None] >= position[None, :]
    )[None]
    scores = (
        jnp.einsum("mthc,muhc->mhtu", query_heads, heads_of_key, preferred_element_type=jnp.float32)
        * scale
    )
    scores = jnp.where(allowed[:, None], scores, masked_score)
    softmax_rows = jnp.exp(scores)
    softmax_rows = softmax_rows / jnp.sum(softmax_rows, -1, keepdims=True)
    soft_low = softmax_rows.astype(jnp.bfloat16)
    attended = (
        jnp.einsum("mhtu,muhc->mthc", soft_low, heads_of_value, preferred_element_type=jnp.float32)
        .astype(jnp.bfloat16)
        .reshape(batch_groups, token_total, head_cols)
    )
    is_last = section_index == section_count - 1

    def select(array, pick):
        return lax.dynamic_index_in_dim(array, pick, 0, keepdims=False)

    def turn_step(turn, carry):
        boundary, grads_now, gain_now, stores_now = carry
        batch = turn - (section_count - 1 - section_index)
        valid = (batch >= 0) & (batch < batch_groups)
        pick = jnp.clip(batch, 0, batch_groups - 1)
        incoming_now = jnp.where(is_last, select(top_rows, pick), boundary)
        upstream_full = lax.all_gather(incoming_now, "tp", axis=0, tiled=True)
        grad_attended = contract_last(upstream_full, out_weight).astype(jnp.bfloat16)
        grad_heads = grad_attended.reshape(token_total, local_heads, HEAD_WIDTH)
        query_now = select(query_heads, pick)
        key_now = select(heads_of_key, pick)
        value_now = select(heads_of_value, pick)
        soft_now = select(softmax_rows, pick)
        soft_low_now = select(soft_low, pick)
        grad_probs = jnp.einsum(
            "thc,uhc->htu", grad_heads, value_now, preferred_element_type=jnp.float32
        )
        grad_scores = soft_now * (grad_probs - jnp.sum(soft_now * grad_probs, -1, keepdims=True))
        scores_low = (grad_scores * scale).astype(jnp.bfloat16)
        grad_query = (
            jnp.einsum("htu,uhc->thc", scores_low, key_now, preferred_element_type=jnp.float32)
            .astype(jnp.bfloat16)
            .reshape(token_total, head_cols)
        )
        key_summands = jnp.einsum(
            "htu,thc->uhc", scores_low, query_now, preferred_element_type=jnp.float32
        )
        value_summands = jnp.einsum(
            "htu,thc->uhc", soft_low_now, grad_heads, preferred_element_type=jnp.float32
        )
        key_cols = jnp.einsum("uhc,hk->ukc", key_summands, pick_wide).reshape(
            token_total, key_width
        )
        value_cols = jnp.einsum("uhc,hk->ukc", value_summands, pick_wide).reshape(
            token_total, key_width
        )
        key_full, value_full = (
            lax.psum(key_cols.astype(jnp.bfloat16), "tp").astype(jnp.float32),
            lax.psum(value_cols.astype(jnp.bfloat16), "tp").astype(jnp.float32),
        )
        key_low = key_full.astype(jnp.bfloat16)
        value_low = value_full.astype(jnp.bfloat16)
        from_queries = lax.psum_scatter(
            contract_last(grad_query, query_weight).astype(jnp.bfloat16),
            "tp",
            scatter_dimension=0,
            tiled=True,
        ).astype(jnp.float32)
        key_slice = (
            contract_last(key_low, key_weight) + contract_last(value_low, value_weight)
        ).astype(jnp.bfloat16)
        from_keys = lax.all_to_all(key_slice, "tp", split_axis=0, concat_axis=1, tiled=True)
        grad_normed = from_queries + from_keys.astype(jnp.float32)
        unit_now = select(own_unit, pick)
        inverse_now = select(own_inverse, pick)
        grad_unit = grad_normed * gain_values
        computed = (
            incoming_now.astype(jnp.float32)
            + inverse_now
            * (grad_unit - unit_now * jnp.mean(grad_unit * unit_now, -1, keepdims=True))
        ).astype(jnp.bfloat16)
        grad_input = jnp.where(valid, computed, jnp.zeros_like(computed))
        grads_now = jnp.where(
            valid, lax.dynamic_update_index_in_dim(grads_now, grad_input, pick, 0), grads_now
        )
        gain_now = gain_now + jnp.where(valid, jnp.sum(grad_normed * unit_now, 0), 0.0)
        normed_now = select(normed, pick)
        cols_now = select(normed_cols, pick)
        attended_now = select(attended, pick)
        terms = (
            jnp.einsum("td,tc->dc", normed_now, grad_query, preferred_element_type=jnp.float32),
            jnp.einsum("td,tc->dc", cols_now, key_low, preferred_element_type=jnp.float32),
            jnp.einsum("td,tc->dc", cols_now, value_low, preferred_element_type=jnp.float32),
            jnp.einsum(
                "tc,td->cd", attended_now, upstream_full, preferred_element_type=jnp.float32
            ),
        )
        stores_now = tuple(
            (older + jnp.where(valid, newer, 0.0) for older, newer in zip(stores_now, terms))
        )
        boundary = passed_along(grad_input, "section", -1)
        return (boundary, grads_now, gain_now, stores_now)

    stores = (
        jnp.zeros((width, head_cols), jnp.float32),
        jnp.zeros((slice_width, key_width), jnp.float32),
        jnp.zeros((slice_width, key_width), jnp.float32),
        jnp.zeros((head_cols, width), jnp.float32),
    )
    start_carry = (
        jnp.zeros((rows, width), jnp.bfloat16),
        jnp.zeros((batch_groups, rows, width), jnp.bfloat16),
        jnp.zeros((width,), jnp.float32),
        stores,
    )
    boundary, grads_in, gain_acc, stores = lax.fori_loop(
        0, section_count + batch_groups - 1, turn_step, start_carry
    )
    grad_query_w, grad_key_w, grad_value_w, grad_out_w = stores
    gain_total = lax.psum(gain_acc.astype(jnp.bfloat16), "tp").astype(jnp.float32)
    return (
        grads_in[None],
        grad_query_w.astype(jnp.bfloat16)[None],
        grad_key_w.astype(jnp.bfloat16)[None],
        grad_value_w.astype(jnp.bfloat16)[None],
        grad_out_w.astype(jnp.bfloat16)[None],
        gain_total[None],
    )


def solution(mesh):
    placed = (
        P("section", None, "tp", None),
        P("section", None),
        P("section", None, "tp"),
        P("section", "tp", None),
        P("section", "tp", None),
        P("section", "tp", None),
        P(None, "tp", None),
        P(None, "tp"),
        P(),
        P(),
        P(),
    )
    return jax.shard_map(
        body,
        mesh=mesh,
        in_specs=placed,
        out_specs=(
            P("section", None, "tp", None),
            P("section", None, "tp"),
            P("section", "tp", None),
            P("section", "tp", None),
            P("section", "tp", None),
            P("section", None),
        ),
        check_vma=False,
    )
```

profile of v0, /device:TPU:0, one launch (start us, length us, event | category | flops | bytes accessed | tf_op | source)
XLA Modules:
  0.0 1200.2 jit_solution(14873112195147949243)
XLA Ops:
  9.8 23.4 %psum.54 = bf16[2,8]{1,0:T(2,128)(2,1)S(1)} all-reduce(bf16[2,8]{1,0:T(2,128)(2,1)S(1)} %convert_element_type.222), channel_id=1, replica_groups=mesh['section'=4,'tp'=8] {'tp'}, use_global_device_ids=true, to_apply=%region_0.0 | all-reduce | flops 16 | bytes 64 | tf_op jit(solution)/shard_map/psum | solution.py:99
  39.3 23.0 %all-gather.4.cloned.1.call-done = bf16[1,2,64,8192]{3,2,1,0:T(8,128)(2,1)} async-done(((bf16[1,2,8,8192]{3,2,1,0:T(8,128)(2,1)}), bf16[1,2,64,8192]{3,2,1,0:T(8,128)(2,1)}) %all-gather.4.cloned.1.call-update) | async-done | bytes 2097168 | tf_op jit(solution)/shard_map/all_gather | solution.py:77
  73.3 5.3 fusion.91
  79.3 64.1 %all-reduce.7.cloned.1.call-done = (bf16[2,64,4,128]{3,2,1,0:T(4,128)(2,1)}, bf16[2,64,4,128]{3,2,1,0:T(4,128)(2,1)}) async-done(((bf16[2,64,4,128]{3,2,1,0:T(4,128)(2,1)}, bf16[2,64,4,128]{3,2,1,0:T(4,128)(2,1)}), (bf16[2,64,4,128]{3,2,1,0:T(4,128)(2,1)}, bf16[2,64,4,128]{3,2,1,0:T(4,128)(2,1)})) %all-reduce.7.cloned.1.call-update) | async-done | bytes 262160 | tf_op jit(solution)/shard_map/psum | solution.py:97
  150.5 985.7 %while.28 = (s32[]{:T(128)}, bf16[8,8192]{1,0:T(8,128)(2,1)S(1)}, bf16[2,8,8192]{2,1,0:T(8,128)(2,1)}, f32[8192]{0:T(1024)S(1)}, f32[8192,512]{1,0:T(8,128)}, /*...) while((s32[]{:T(128)}, bf16[8,8192]{1,0:T(8,128)(2,1)S(1)}, ...), condition=%wide.region_13.14_spmd.clone, body=%wide.region_6.13_spmd.clone.sunk | while | flops 2463810304 | bytes 129438680 | solution.py:240
  153.1 39.9 %all-gather.6.cloned.1.call-done = bf16[64,8192]{1,0:T(8,128)(2,1)} async-done(((bf16[8,8192]{1,0:T(8,128)(2,1)}), bf16[64,8192]{1,0:T(8,128)(2,1)}) %all-gather.6.cloned.1.call-update) | async-done | bytes 1048592 | tf_op jit(solution)/shard_map/while/body/eval_jaxpr/all_gather | solution.py:151
  193.0 6.4 fusion.211
  203.7 7.1 convolution_convert_fusion.15
  210.8 9.1 select_add_fusion.14
  219.9 7.1 select_add_fusion.11
  227.0 46.3 %all-reduce.9.cloned.1.call-done = (bf16[64,512]{1,0:T(8,128)(2,1)}, bf16[64,512]{1,0:T(8,128)(2,1)}) async-done(((bf16[64,512]{1,0:T(8,128)(2,1)}, bf16[64,512]{1,0:T(8,128)(2,1)}), (bf16[64,512]{1,0:T(8,128)(2,1)}, bf16[64,512]{1,0:T(8,128)(2,1)})) %all-reduce.9.cloned.1.call-update) | async-done | bytes 131088 | tf_op jit(solution)/shard_map/while/body/eval_jaxpr/psum | solution.py:182
  275.0 2.4 fusion.216
  277.3 3.7 all-to-all-start
  282.7 2.7 select_add_fusion.12
  285.4 3.5 all-to-all-done
  288.9 51.6 %reduce-scatter.2.cloned.1.call-done = bf16[8,8192]{1,0:T(8,128)(2,1)} async-done(((bf16[64,8192]{1,0:T(8,128)(2,1)}), bf16[8,8192]{1,0:T(8,128)(2,1)}) %reduce-scatter.2.cloned.1.call-update) | async-done | bytes 131088 | tf_op jit(solution)/shard_map/while/body/eval_jaxpr/reduce_scatter | solution.py:187
  349.2 41.1 %all-gather.6.cloned.1.call-done = bf16[64,8192]{1,0:T(8,128)(2,1)} async-done(((bf16[8,8192]{1,0:T(8,128)(2,1)}), bf16[64,8192]{1,0:T(8,128)(2,1)}) %all-gather.6.cloned.1.call-update) | async-done | bytes 1048592 | tf_op jit(solution)/shard_map/while/body/eval_jaxpr/all_gather | solution.py:151
  390.3 6.4 fusion.211
  401.0 7.1 convolution_convert_fusion.15
  408.1 14.1 %select_add_fusion.14 = f32[512,8192]{1,0:T(8,128)} fusion(f32[512,8192]{1,0:T(8,128)} %get-tuple-element.1036, bf16[64,8192]{1,0:T(8,128)(2,1)S(1)} %copy-done.2, pred[]{:T(512)S(6)} %compare.10, pred[]{:T(512)S(6)} %and.44, bf16[2,64,512]{2,1,0:T(8,128)(2,1)} %get-tuple-element.1084, s32[]{:T(128)S(6)} %min.12), kind=kOutput, calls=%fused_computation.2.clone.1 | convolution fusion | flops 549453824 | bytes 34668552 | tf_op jit(solution)/shard_map/while/body/eval_jaxpr/tc,td->cd/dot_general | solution.py:218
  422.2 10.6 select_add_fusion.11
  432.8 37.7 %all-reduce.9.cloned.1.call-done = (bf16[64,512]{1,0:T(8,128)(2,1)}, bf16[64,512]{1,0:T(8,128)(2,1)}) async-done(((bf16[64,512]{1,0:T(8,128)(2,1)}, bf16[64,512]{1,0:T(8,128)(2,1)}), (bf16[64,512]{1,0:T(8,128)(2,1)}, bf16[64,512]{1,0:T(8,128)(2,1)})) %all-reduce.9.cloned.1.call-update) | async-done | bytes 131088 | tf_op jit(solution)/shard_map/while/body/eval_jaxpr/psum | solution.py:182
  472.2 2.4 fusion.216
  474.6 3.7 all-to-all-start
  479.9 3.5 select_add_fusion.12
  483.5 2.3 all-to-all-done
  485.8 52.1 %reduce-scatter.2.cloned.1.call-done = bf16[8,8192]{1,0:T(8,128)(2,1)} async-done(((bf16[64,8192]{1,0:T(8,128)(2,1)}), bf16[8,8192]{1,0:T(8,128)(2,1)}) %reduce-scatter.2.cloned.1.call-update) | async-done | bytes 131088 | tf_op jit(solution)/shard_map/while/body/eval_jaxpr/reduce_scatter | solution.py:187
  546.7 41.4 %all-gather.6.cloned.1.call-done = bf16[64,8192]{1,0:T(8,128)(2,1)} async-done(((bf16[8,8192]{1,0:T(8,128)(2,1)}), bf16[64,8192]{1,0:T(8,128)(2,1)}) %all-gather.6.cloned.1.call-update) | async-done | bytes 1048592 | tf_op jit(solution)/shard_map/while/body/eval_jaxpr/all_gather | solution.py:151
  588.0 6.4 fusion.211
  598.7 7.1 convolution_convert_fusion.15
  605.8 14.1 %select_add_fusion.14 = f32[512,8192]{1,0:T(8,128)} fusion(f32[512,8192]{1,0:T(8,128)} %get-tuple-element.1036, bf16[64,8192]{1,0:T(8,128)(2,1)S(1)} %copy-done.2, pred[]{:T(512)S(6)} %compare.10, pred[]{:T(512)S(6)} %and.44, bf16[2,64,512]{2,1,0:T(8,128)(2,1)} %get-tuple-element.1084, s32[]{:T(128)S(6)} %min.12), kind=kOutput, calls=%fused_computation.2.clone.1 | convolution fusion | flops 549453824 | bytes 34668552 | tf_op jit(solution)/shard_map/while/body/eval_jaxpr/tc,td->cd/dot_general | solution.py:218
  620.0 10.6 select_add_fusion.11
  630.6 37.7 %all-reduce.9.cloned.1.call-done = (bf16[64,512]{1,0:T(8,128)(2,1)}, bf16[64,512]{1,0:T(8,128)(2,1)}) async-done(((bf16[64,512]{1,0:T(8,128)(2,1)}, bf16[64,512]{1,0:T(8,128)(2,1)}), (bf16[64,512]{1,0:T(8,128)(2,1)}, bf16[64,512]{1,0:T(8,128)(2,1)})) %all-reduce.9.cloned.1.call-update) | async-done | bytes 131088 | tf_op jit(solution)/shard_map/while/body/eval_jaxpr/psum | solution.py:182
  670.0 2.4 fusion.216
  672.4 3.7 all-to-all-start
  677.7 3.5 select_add_fusion.12
  681.2 2.3 all-to-all-done
  683.6 51.9 %reduce-scatter.2.cloned.1.call-done = bf16[8,8192]{1,0:T(8,128)(2,1)} async-done(((bf16[64,8192]{1,0:T(8,128)(2,1)}), bf16[8,8192]{1,0:T(8,128)(2,1)}) %reduce-scatter.2.cloned.1.call-update) | async-done | bytes 131088 | tf_op jit(solution)/shard_map/while/body/eval_jaxpr/reduce_scatter | solution.py:187
  744.2 41.1 %all-gather.6.cloned.1.call-done = bf16[64,8192]{1,0:T(8,128)(2,1)} async-done(((bf16[8,8192]{1,0:T(8,128)(2,1)}), bf16[64,8192]{1,0:T(8,128)(2,1)}) %all-gather.6.cloned.1.call-update) | async-done | bytes 1048592 | tf_op jit(solution)/shard_map/while/body/eval_jaxpr/all_gather | solution.py:151
  785.3 6.4 fusion.211
  796.0 7.1 convolution_convert_fusion.15
  803.1 14.1 %select_add_fusion.14 = f32[512,8192]{1,0:T(8,128)} fusion(f32[512,8192]{1,0:T(8,128)} %get-tuple-element.1036, bf16[64,8192]{1,0:T(8,128)(2,1)S(1)} %copy-done.2, pred[]{:T(512)S(6)} %compare.10, pred[]{:T(512)S(6)} %and.44, bf16[2,64,512]{2,1,0:T(8,128)(2,1)} %get-tuple-element.1084, s32[]{:T(128)S(6)} %min.12), kind=kOutput, calls=%fused_computation.2.clone.1 | convolution fusion | flops 549453824 | bytes 34668552 | tf_op jit(solution)/shard_map/while/body/eval_jaxpr/tc,td->cd/dot_general | solution.py:218
  817.2 10.6 select_add_fusion.11
  827.8 37.7 %all-reduce.9.cloned.1.call-done = (bf16[64,512]{1,0:T(8,128)(2,1)}, bf16[64,512]{1,0:T(8,128)(2,1)}) async-done(((bf16[64,512]{1,0:T(8,128)(2,1)}, bf16[64,512]{1,0:T(8,128)(2,1)}), (bf16[64,512]{1,0:T(8,128)(2,1)}, bf16[64,512]{1,0:T(8,128)(2,1)})) %all-reduce.9.cloned.1.call-update) | async-done | bytes 131088 | tf_op jit(solution)/shard_map/while/body/eval_jaxpr/psum | solution.py:182
  867.2 2.4 fusion.216
  869.6 3.7 all-to-all-start
  875.0 3.5 select_add_fusion.12
  878.5 2.7 all-to-all-done
  881.1 51.6 %reduce-scatter.2.cloned.1.call-done = bf16[8,8192]{1,0:T(8,128)(2,1)} async-done(((bf16[64,8192]{1,0:T(8,128)(2,1)}), bf16[8,8192]{1,0:T(8,128)(2,1)}) %reduce-scatter.2.cloned.1.call-update) | async-done | bytes 131088 | tf_op jit(solution)/shard_map/while/body/eval_jaxpr/reduce_scatter | solution.py:187
  941.5 41.1 %all-gather.6.cloned.1.call-done = bf16[64,8192]{1,0:T(8,128)(2,1)} async-done(((bf16[8,8192]{1,0:T(8,128)(2,1)}), bf16[64,8192]{1,0:T(8,128)(2,1)}) %all-gather.6.cloned.1.call-update) | async-done | bytes 1048592 | tf_op jit(solution)/shard_map/while/body/eval_jaxpr/all_gather | solution.py:151
  982.5 6.4 fusion.211
  993.3 7.1 convolution_convert_fusion.15
  1000.4 14.1 %select_add_fusion.14 = f32[512,8192]{1,0:T(8,128)} fusion(f32[512,8192]{1,0:T(8,128)} %get-tuple-element.1036, bf16[64,8192]{1,0:T(8,128)(2,1)S(1)} %copy-done.2, pred[]{:T(512)S(6)} %compare.10, pred[]{:T(512)S(6)} %and.44, bf16[2,64,512]{2,1,0:T(8,128)(2,1)} %get-tuple-element.1084, s32[]{:T(128)S(6)} %min.12), kind=kOutput, calls=%fused_computation.2.clone.1 | convolution fusion | flops 549453824 | bytes 34668552 | tf_op jit(solution)/shard_map/while/body/eval_jaxpr/tc,td->cd/dot_general | solution.py:218
  1014.5 10.6 select_add_fusion.11
  1025.1 37.7 %all-reduce.9.cloned.1.call-done = (bf16[64,512]{1,0:T(8,128)(2,1)}, bf16[64,512]{1,0:T(8,128)(2,1)}) async-done(((bf16[64,512]{1,0:T(8,128)(2,1)}, bf16[64,512]{1,0:T(8,128)(2,1)}), (bf16[64,512]{1,0:T(8,128)(2,1)}, bf16[64,512]{1,0:T(8,128)(2,1)})) %all-reduce.9.cloned.1.call-update) | async-done | bytes 131088 | tf_op jit(solution)/shard_map/while/body/eval_jaxpr/psum | solution.py:182
  1064.5 2.4 fusion.216
  1066.9 3.7 all-to-all-start
  1072.2 3.5 select_add_fusion.12
  1075.7 2.7 all-to-all-done
  1078.4 51.6 %reduce-scatter.2.cloned.1.call-done = bf16[8,8192]{1,0:T(8,128)(2,1)} async-done(((bf16[64,8192]{1,0:T(8,128)(2,1)}), bf16[8,8192]{1,0:T(8,128)(2,1)}) %reduce-scatter.2.cloned.1.call-update) | async-done | bytes 131088 | tf_op jit(solution)/shard_map/while/body/eval_jaxpr/reduce_scatter | solution.py:187
  1137.4 35.1 %psum.57 = bf16[1,8192]{1,0:T(2,128)(2,1)S(1)} all-reduce(bf16[1,8192]{1,0:T(2,128)(2,1)S(1)} %broadcast_in_dim.133), channel_id=1, replica_groups=mesh['section'=4,'tp'=8] {'tp'}, use_global_device_ids=true, to_apply=%region_14.15 | all-reduce | flops 8192 | bytes 32768 | tf_op jit(solution)/shard_map/psum | solution.py:244
  1173.1 2.7 convert_bitcast_fusion.3
  1175.8 8.9 convert_bitcast_fusion
  1184.7 9.0 convert_bitcast_fusion.1
  (232 shorter events, 110.9 us)
Async XLA Ops:
  7.2 1.6 copy-start
  7.2 55.1 %all-gather.4.cloned.1.call-start = ((), (), s32[]{:S(2)}) async-start(), calls=%async_computation.2 | async-start | bytes 2359296 | tf_op jit(solution)/shard_map/all_gather | solution.py:77
  7.9 135.4 %all-reduce.7.cloned.1.call-start = ((), (), s32[]{:S(2)}) async-start(), calls=%async_computation.3 | async-start | bytes 524288 | tf_op jit(solution)/shard_map/psum | solution.py:97
  66.6 1.3 copy-start.3
  150.5 42.5 %all-gather.6.cloned.1.call-start = ((), (), s32[]{:S(2)}) async-start(), calls=%async_computation.4 | async-start | bytes 1179648 | tf_op jit(solution)/shard_map/while/body/eval_jaxpr/all_gather | solution.py:151
  152.1 121.1 %all-reduce.9.cloned.1.call-start = ((), (), s32[]{:S(2)}) async-start(), calls=%async_computation.5 | async-start | bytes 262144 | tf_op jit(solution)/shard_map/while/body/eval_jaxpr/psum | solution.py:182
  203.6 136.8 %reduce-scatter.2.cloned.1.call-start = ((), (), s32[]{:S(2)}) async-start(), calls=%async_computation.6 | async-start | bytes 1179648 | tf_op jit(solution)/shard_map/while/body/eval_jaxpr/reduce_scatter | solution.py:187
  203.7 7.1 copy-start.2
  210.8 9.1 copy-start.4
  273.2 9.4 copy-start.7
  277.3 11.5 all-to-all-start
  281.0 59.5 %copy-start.6 = (f32[2,8,8192]{2,1,0:T(8,128)S(1)}, f32[2,8,8192]{2,1,0:T(8,128)}, u32[]{:S(2)}) copy-start(f32[2,8,8192]{2,1,0:T(8,128)} %get-tuple-element.1081) | copy-start | bytes 1572868 | tf_op jit(solution)/shard_map/while
  281.0 60.6 %copy-start.5 = (bf16[8,8192]{1,0:T(8,128)(2,1)S(1)}, bf16[8,8192]{1,0:T(8,128)(2,1)}, u32[]{:S(2)}) copy-start(bf16[8,8192]{1,0:T(8,128)(2,1)} %bitcast_select_fusion.3) | copy-start | bytes 393220 | tf_op jit(solution)/shard_map/while
  343.4 3.2 collective-permute-start
  346.7 43.6 %all-gather.6.cloned.1.call-start = ((), (), s32[]{:S(2)}) async-start(), calls=%async_computation.4 | async-start | bytes 1179648 | tf_op jit(solution)/shard_map/while/body/eval_jaxpr/all_gather | solution.py:151
  348.3 122.2 %all-reduce.9.cloned.1.call-start = ((), (), s32[]{:S(2)}) async-start(), calls=%async_computation.5 | async-start | bytes 262144 | tf_op jit(solution)/shard_map/while/body/eval_jaxpr/psum | solution.py:182
  400.9 137.0 %reduce-scatter.2.cloned.1.call-start = ((), (), s32[]{:S(2)}) async-start(), calls=%async_computation.6 | async-start | bytes 1179648 | tf_op jit(solution)/shard_map/while/body/eval_jaxpr/reduce_scatter | solution.py:187
  401.0 7.1 copy-start.2
  408.1 14.1 %copy-start.4 = (bf16[2,64,8192]{2,1,0:T(8,128)(2,1)S(1)}, bf16[2,64,8192]{2,1,0:T(8,128)(2,1)}, u32[]{:S(2)}) copy-start(bf16[2,64,8192]{2,1,0:T(8,128)(2,1)} %get-tuple-element.1082) | copy-start | bytes 6291460 | tf_op jit(solution)/shard_map/while
  470.5 9.4 copy-start.7
  474.6 11.2 all-to-all-start
  478.3 59.6 %copy-start.6 = (f32[2,8,8192]{2,1,0:T(8,128)S(1)}, f32[2,8,8192]{2,1,0:T(8,128)}, u32[]{:S(2)}) copy-start(f32[2,8,8192]{2,1,0:T(8,128)} %get-tuple-element.1081) | copy-start | bytes 1572868 | tf_op jit(solution)/shard_map/while
  478.3 60.8 %copy-start.5 = (bf16[8,8192]{1,0:T(8,128)(2,1)S(1)}, bf16[8,8192]{1,0:T(8,128)(2,1)}, u32[]{:S(2)}) copy-start(bf16[8,8192]{1,0:T(8,128)(2,1)} %bitcast_select_fusion.3) | copy-start | bytes 393220 | tf_op jit(solution)/shard_map/while
  540.9 3.2 collective-permute-start
  544.1 43.9 %all-gather.6.cloned.1.call-start = ((), (), s32[]{:S(2)}) async-start(), calls=%async_computation.4 | async-start | bytes 1179648 | tf_op jit(solution)/shard_map/while/body/eval_jaxpr/all_gather | solution.py:151
  545.7 122.6 %all-reduce.9.cloned.1.call-start = ((), (), s32[]{:S(2)}) async-start(), calls=%async_computation.5 | async-start | bytes 262144 | tf_op jit(solution)/shard_map/while/body/eval_jaxpr/psum | solution.py:182
  598.7 136.8 %reduce-scatter.2.cloned.1.call-start = ((), (), s32[]{:S(2)}) async-start(), calls=%async_computation.6 | async-start | bytes 1179648 | tf_op jit(solution)/shard_map/while/body/eval_jaxpr/reduce_scatter | solution.py:187
  598.7 7.1 copy-start.2
  605.8 14.1 %copy-start.4 = (bf16[2,64,8192]{2,1,0:T(8,128)(2,1)S(1)}, bf16[2,64,8192]{2,1,0:T(8,128)(2,1)}, u32[]{:S(2)}) copy-start(bf16[2,64,8192]{2,1,0:T(8,128)(2,1)} %get-tuple-element.1082) | copy-start | bytes 6291460 | tf_op jit(solution)/shard_map/while
  668.2 9.4 copy-start.7
  672.4 11.2 all-to-all-start
  676.0 59.5 %copy-start.6 = (f32[2,8,8192]{2,1,0:T(8,128)S(1)}, f32[2,8,8192]{2,1,0:T(8,128)}, u32[]{:S(2)}) copy-start(f32[2,8,8192]{2,1,0:T(8,128)} %get-tuple-element.1081) | copy-start | bytes 1572868 | tf_op jit(solution)/shard_map/while
  676.0 60.6 %copy-start.5 = (bf16[8,8192]{1,0:T(8,128)(2,1)S(1)}, bf16[8,8192]{1,0:T(8,128)(2,1)}, u32[]{:S(2)}) copy-start(bf16[8,8192]{1,0:T(8,128)(2,1)} %bitcast_select_fusion.3) | copy-start | bytes 393220 | tf_op jit(solution)/shard_map/while
  738.4 3.2 collective-permute-start
  741.7 43.6 %all-gather.6.cloned.1.call-start = ((), (), s32[]{:S(2)}) async-start(), calls=%async_computation.4 | async-start | bytes 1179648 | tf_op jit(solution)/shard_map/while/body/eval_jaxpr/all_gather | solution.py:151
  743.3 122.2 %all-reduce.9.cloned.1.call-start = ((), (), s32[]{:S(2)}) async-start(), calls=%async_computation.5 | async-start | bytes 262144 | tf_op jit(solution)/shard_map/while/body/eval_jaxpr/psum | solution.py:182
  795.9 136.8 %reduce-scatter.2.cloned.1.call-start = ((), (), s32[]{:S(2)}) async-start(), calls=%async_computation.6 | async-start | bytes 1179648 | tf_op jit(solution)/shard_map/while/body/eval_jaxpr/reduce_scatter | solution.py:187
  796.0 7.1 copy-start.2
  803.1 14.1 %copy-start.4 = (bf16[2,64,8192]{2,1,0:T(8,128)(2,1)S(1)}, bf16[2,64,8192]{2,1,0:T(8,128)(2,1)}, u32[]{:S(2)}) copy-start(bf16[2,64,8192]{2,1,0:T(8,128)(2,1)} %get-tuple-element.1082) | copy-start | bytes 6291460 | tf_op jit(solution)/shard_map/while
  865.5 9.4 copy-start.7
  869.6 11.5 all-to-all-start
  873.3 59.4 %copy-start.6 = (f32[2,8,8192]{2,1,0:T(8,128)S(1)}, f32[2,8,8192]{2,1,0:T(8,128)}, u32[]{:S(2)}) copy-start(f32[2,8,8192]{2,1,0:T(8,128)} %get-tuple-element.1081) | copy-start | bytes 1572868 | tf_op jit(solution)/shard_map/while
  873.3 60.6 %copy-start.5 = (bf16[8,8192]{1,0:T(8,128)(2,1)S(1)}, bf16[8,8192]{1,0:T(8,128)(2,1)}, u32[]{:S(2)}) copy-start(bf16[8,8192]{1,0:T(8,128)(2,1)} %bitcast_select_fusion.3) | copy-start | bytes 393220 | tf_op jit(solution)/shard_map/while
  935.7 3.2 collective-permute-start
  938.9 43.6 %all-gather.6.cloned.1.call-start = ((), (), s32[]{:S(2)}) async-start(), calls=%async_computation.4 | async-start | bytes 1179648 | tf_op jit(solution)/shard_map/while/body/eval_jaxpr/all_gather | solution.py:151
  940.5 122.2 %all-reduce.9.cloned.1.call-start = ((), (), s32[]{:S(2)}) async-start(), calls=%async_computation.5 | async-start | bytes 262144 | tf_op jit(solution)/shard_map/while/body/eval_jaxpr/psum | solution.py:182
  993.2 136.8 %reduce-scatter.2.cloned.1.call-start = ((), (), s32[]{:S(2)}) async-start(), calls=%async_computation.6 | async-start | bytes 1179648 | tf_op jit(solution)/shard_map/while/body/eval_jaxpr/reduce_scatter | solution.py:187
  993.3 7.1 copy-start.2
  1000.4 14.1 %copy-start.4 = (bf16[2,64,8192]{2,1,0:T(8,128)(2,1)S(1)}, bf16[2,64,8192]{2,1,0:T(8,128)(2,1)}, u32[]{:S(2)}) copy-start(bf16[2,64,8192]{2,1,0:T(8,128)(2,1)} %get-tuple-element.1082) | copy-start | bytes 6291460 | tf_op jit(solution)/shard_map/while
  1062.8 9.4 copy-start.7
  1066.9 11.5 all-to-all-start
  1070.6 59.5 %copy-start.6 = (f32[2,8,8192]{2,1,0:T(8,128)S(1)}, f32[2,8,8192]{2,1,0:T(8,128)}, u32[]{:S(2)}) copy-start(f32[2,8,8192]{2,1,0:T(8,128)} %get-tuple-element.1081) | copy-start | bytes 1572868 | tf_op jit(solution)/shard_map/while
  1070.6 60.6 %copy-start.5 = (bf16[8,8192]{1,0:T(8,128)(2,1)S(1)}, bf16[8,8192]{1,0:T(8,128)(2,1)}, u32[]{:S(2)}) copy-start(bf16[8,8192]{1,0:T(8,128)(2,1)} %bitcast_select_fusion.3) | copy-start | bytes 393220 | tf_op jit(solution)/shard_map/while
  1133.0 3.2 collective-permute-start
  1184.7 9.0 copy-start.1
Sparse Core Ops, SparseCore 0:
  10.2 52.0 all-gather.3
  73.4 69.8 all-reduce.6
  153.4 39.5 all-gather.5
  203.8 69.4 all-reduce.8
  277.1 63.3 reduce-scatter.1
  349.3 40.9 all-gather.5
  401.0 69.4 all-reduce.8
  474.5 63.3 reduce-scatter.1
  547.0 40.9 all-gather.5
  598.8 69.4 all-reduce.8
  672.2 63.2 reduce-scatter.1
  744.3 40.9 all-gather.5
  796.1 69.4 all-reduce.8
  869.4 63.3 reduce-scatter.1
  941.6 40.9 all-gather.5
  993.3 69.4 all-reduce.8
  1066.6 63.3 reduce-scatter.1
where the time goes:
time: 1200 us
  waiting for transfers between devices  771 us (64%)
  matrix products  260 us (22%)
  blocking collectives  58.5 us (5%)
  other arithmetic  54.8 us (5%)
  starting transfers between devices  25.3 us (2%)
  local copies, waits for them, and re-layouts  15.9 us (1%)
  between operations  13.9 us (1%)
    reduce_scatter x5, waiting for transfers between devices, turn_step(): lax.psum_scatter(contract_last(grad_query, query_weight).astype(jnp.bfloa...  259 us
    all_gather x5, waiting for transfers between devices, turn_step(): upstream_full = lax.all_gather(incoming_now, 'tp', axis=0, tiled=True)  204 us
    psum x5, waiting for transfers between devices, turn_step(): lax.psum(key_cols.astype(jnp.bfloat16), 'tp').astype(jnp.float32)  197 us
    dot_general x20, matrix products, contract_last(): lax.dot_general(left, right, (((1,), (1,)), ((), ())), preferred_element_...  87.8 us
    dot_general x5, matrix products, turn_step(): jnp.einsum('tc,td->cd', attended_now, upstream_full, preferred_element_ty...  65.5 us
    psum x1, waiting for transfers between devices, body(): lax.psum(key_part.astype(jnp.bfloat16), 'tp').astype(jnp.float32)  64.1 us
    dot_general x5, matrix products, turn_step(): jnp.einsum('td,tc->dc', normed_now, grad_query, preferred_element_type=jn...  49.5 us
    psum x1, blocking collectives, body(): lax.psum(gain_acc.astype(jnp.bfloat16), 'tp').astype(jnp.float32)  35.1 us
  transfers between devices with their start and end apart: 27, of which 27 were waited for; matrix products, arithmetic and copies ran while one was open for 18% of the time, Pallas kernels for 0%

commit v1 on v0

v1 whole, which is shorter than its diff:
```python
import functools
import math

import jax
import jax.numpy as jnp
from jax import lax
from jax.experimental import pallas as pl
from jax.experimental.pallas import tpu as pltpu
from jax.sharding import PartitionSpec as P

HEAD_WIDTH = 128
QUERY_HEAD_COUNT = 32
SLOTS = 4


norm_epsilon = 1e-05
pair_beta = 4.0
masked_score = -1e30


def pair_weights(seq_sums, pair_of_slot, pair_counts):
    table = (
        pair_of_slot[:, :, None] == jnp.arange(pair_counts.shape[0], dtype=jnp.int32)[None, None, :]
    ).astype(jnp.float32)
    counts = jnp.einsum("msp,pc->msc", table, pair_counts.astype(jnp.float32))
    margin = pair_beta * (seq_sums[:, 0::2] / counts[:, :, 0] - seq_sums[:, 1::2] / counts[:, :, 1])
    weight = pair_beta * jax.nn.sigmoid(-margin)
    stacked = jnp.stack([-weight / counts[:, :, 0], weight / counts[:, :, 1]], -1)
    return stacked.reshape(seq_sums.shape)


def contract_last(left, right):
    return lax.dot_general(
        left, right, (((1,), (1,)), ((), ())), preferred_element_type=jnp.float32
    )


MESH = pl.DeviceIdType.MESH
VMEM_LIMIT = 48 * 1024 * 1024


def exchange_kernel(kinds, tp_count, group, section_count, *refs):
    count = len(kinds)
    ins, outs = refs[:count], refs[count : 2 * count]
    send_sem, recv_sem = refs[2 * count :]
    sec = lax.axis_index("section")
    me = lax.axis_index("tp")
    barrier = pltpu.get_barrier_semaphore()
    for d in range(1, tp_count):
        pl.semaphore_signal(
            barrier, inc=1, device_id=(sec, lax.rem(me + d, tp_count)), device_id_type=MESH
        )
    pl.semaphore_wait(barrier, tp_count - 1)

    def copies(a):
        made = []
        for d in range(1, tp_count):
            peer = lax.rem(me + d, tp_count)
            source = ins[a].at[peer // group] if kinds[a] == "pick" else ins[a]
            made.append(
                pltpu.make_async_remote_copy(
                    src_ref=source,
                    dst_ref=outs[a].at[me],
                    send_sem=send_sem.at[a, d],
                    recv_sem=recv_sem.at[a, d],
                    device_id=(sec, peer),
                    device_id_type=MESH,
                )
            )
        return made

    def send(a):
        for copy in copies(a):
            copy.start()
        outs[a][me] = ins[a][me // group] if kinds[a] == "pick" else ins[a][...]

    def receive(a):
        for copy in copies(a):
            copy.wait()

    for step in (send, receive):
        for a in range(count):
            if kinds[a] == "last":
                pl.when(sec == section_count - 1)(functools.partial(step, a))
            else:
                step(a)


def exchange(arrays, kinds, group, identity):
    tp_count = lax.axis_size("tp")
    shapes = [
        jax.ShapeDtypeStruct(
            (tp_count,) + (a.shape[1:] if kind == "pick" else a.shape), a.dtype
        )
        for a, kind in zip(arrays, kinds)
    ]
    vmem = pl.BlockSpec(memory_space=pltpu.VMEM)
    return pl.pallas_call(
        functools.partial(exchange_kernel, kinds, tp_count, group, lax.axis_size("section")),
        out_shape=shapes,
        in_specs=[vmem] * len(arrays),
        out_specs=[vmem] * len(arrays),
        scratch_shapes=[
            pltpu.SemaphoreType.DMA((len(arrays), tp_count)),
            pltpu.SemaphoreType.DMA((len(arrays), tp_count)),
        ],
        compiler_params=pltpu.CompilerParams(
            collective_id=identity, has_side_effects=True, vmem_limit_bytes=VMEM_LIMIT
        ),
        name=f"exchange_{identity}",
    )(*arrays)


def relay_kernel(
    turn,
    batch_groups,
    section_count,
    tp_count,
    part_ref,
    dkv_ref,
    g_ref,
    saved_ref,
    gain_ref,
    kw_ref,
    vw_ref,
    gin_ref,
    gnext_ref,
    dkv_full_ref,
    gain_out_ref,
    part_recv,
    dkv_recv,
    ks_send,
    ks_recv,
    grad_unit,
    unit,
    p_send,
    p_recv,
    d_send,
    d_recv,
    k_send,
    k_recv,
    g_send,
    g_recv,
):
    sec = lax.axis_index("section")
    me = lax.axis_index("tp")
    rows, width = gin_ref.shape
    slice_width = kw_ref.shape[0]
    key_width = kw_ref.shape[1]
    key_count = key_width // HEAD_WIDTH
    sharers = tp_count // key_count
    first = section_count - 1 - turn
    active = (sec >= first) & (sec < first + batch_groups)
    fed = (sec + 1 >= first) & (sec + 1 < first + batch_groups) & (sec < section_count - 1)
    feeds = active & (sec > 0)
    barrier = pltpu.get_barrier_semaphore()

    def peer(d):
        return lax.rem(me + d, tp_count)

    @pl.when(active)
    def _():
        for d in range(1, tp_count):
            pl.semaphore_signal(barrier, inc=1, device_id=(sec, peer(d)), device_id_type=MESH)

    @pl.when(fed)
    def _():
        for d in range(tp_count):
            pl.semaphore_signal(barrier, inc=1, device_id=(sec + 1, peer(d)), device_id_type=MESH)

    def remote(source, target, sends, receives, d, section):
        return pltpu.make_async_remote_copy(
            src_ref=source,
            dst_ref=target,
            send_sem=sends.at[d],
            recv_sem=receives.at[d],
            device_id=(section, peer(d)),
            device_id_type=MESH,
        )

    def part_copy(d):
        return remote(part_ref.at[peer(d)], part_recv.at[me], p_send, p_recv, d, sec)

    def dkv_copy(d):
        return remote(dkv_ref, dkv_recv.at[me], d_send, d_recv, d, sec)

    def ks_copy(d):
        return remote(ks_send.at[peer(d)], ks_recv.at[me], k_send, k_recv, d, sec)

    @pl.when(feeds)
    def _():
        pl.semaphore_wait(barrier, 2 * tp_count - 1)

    @pl.when(active & (sec == 0))
    def _():
        pl.semaphore_wait(barrier, tp_count - 1)

    @pl.when(active)
    def _():
        for d in range(1, tp_count):
            dkv_copy(d).start()
        for d in range(1, tp_count):
            part_copy(d).start()
        dkv_recv[me] = dkv_ref[...]
        part_recv[me] = part_ref[me]
        x = saved_ref[...].astype(jnp.float32)
        inverse = lax.rsqrt(jnp.mean(x * x, -1, keepdims=True) + norm_epsilon)
        unit[...] = x * inverse
        for d in range(1, tp_count):
            dkv_copy(d).wait()
        for kind in range(2):
            for k in range(key_count):
                total = dkv_recv[k * sharers, kind].astype(jnp.float32)
                for other in range(1, sharers):
                    total = total + dkv_recv[k * sharers + other, kind].astype(jnp.float32)
                dkv_full_ref[kind, :, k * HEAD_WIDTH : (k + 1) * HEAD_WIDTH] = total.astype(
                    jnp.bfloat16
                )
        key_slice = contract_last(dkv_full_ref[0], kw_ref[...]) + contract_last(
            dkv_full_ref[1], vw_ref[...]
        )
        for j in range(tp_count):
            ks_send[j] = key_slice[j * rows : (j + 1) * rows].astype(jnp.bfloat16)
        for d in range(1, tp_count):
            ks_copy(d).start()
        ks_recv[me] = ks_send[me]
        for d in range(1, tp_count):
            part_copy(d).wait()
        for d in range(1, tp_count):
            ks_copy(d).wait()
        dots = jnp.zeros((rows, 1), jnp.float32)
        for i in range(tp_count):
            cols = slice(i * slice_width, (i + 1) * slice_width)
            normed_grad = ks_recv[i].astype(jnp.float32) + jnp.sum(
                part_recv[:, :, cols].astype(jnp.float32), 0
            )
            unit_part = unit[:, cols]
            gain_out_ref[:, cols] = jnp.sum(normed_grad * unit_part, 0, keepdims=True)
            scaled = normed_grad * gain_ref[:, cols].astype(jnp.float32)
            grad_unit[:, cols] = scaled
            dots = dots + jnp.sum(scaled * unit_part, -1, keepdims=True)
        dots = dots / width
        for i in range(tp_count):
            cols = slice(i * slice_width, (i + 1) * slice_width)
            gin_ref[:, cols] = (
                g_ref[me, :, cols].astype(jnp.float32)
                + inverse * (grad_unit[:, cols] - unit[:, cols] * dots)
            ).astype(jnp.bfloat16)

    @pl.when(feeds)
    def _():
        for d in range(tp_count):
            remote(gin_ref, gnext_ref.at[me], g_send, g_recv, d, sec - 1).start()
        for d in range(tp_count):
            remote(gin_ref, gnext_ref.at[me], g_send, g_recv, d, sec - 1).wait_send()

    @pl.when(fed)
    def _():
        for d in range(tp_count):
            remote(gin_ref, gnext_ref.at[me], g_send, g_recv, d, sec).wait_recv()


def relay(turn, batch_groups, identity, part, dkv, g, saved, gain, kw, vw):
    tp_count, rows, width = part.shape
    tokens = dkv.shape[1]
    slice_width, key_width = kw.shape
    vmem = pl.BlockSpec(memory_space=pltpu.VMEM)
    dma = pltpu.SemaphoreType.DMA((tp_count,))
    low = jnp.bfloat16
    return pl.pallas_call(
        functools.partial(relay_kernel, turn, batch_groups, lax.axis_size("section"), tp_count),
        out_shape=[
            jax.ShapeDtypeStruct((rows, width), low),
            jax.ShapeDtypeStruct((tp_count, rows, width), low),
            jax.ShapeDtypeStruct((2, tokens, key_width), low),
            jax.ShapeDtypeStruct((1, width), jnp.float32),
        ],
        in_specs=[vmem] * 7,
        out_specs=[vmem] * 4,
        scratch_shapes=[
            pltpu.VMEM((tp_count, rows, width), low),
            pltpu.VMEM((tp_count, 2, tokens, HEAD_WIDTH), low),
            pltpu.VMEM((tp_count, rows, slice_width), low),
            pltpu.VMEM((tp_count, rows, slice_width), low),
            pltpu.VMEM((rows, width), jnp.float32),
            pltpu.VMEM((rows, width), jnp.float32),
        ]
        + [dma] * 8,
        compiler_params=pltpu.CompilerParams(
            collective_id=identity, has_side_effects=True, vmem_limit_bytes=VMEM_LIMIT
        ),
        name=f"relay_{turn}",
    )(*lax.optimization_barrier((part, dkv, g, saved, gain, kw, vw)))


def body(
    section_inputs,
    norm_gain,
    w_query,
    key_projection,
    value_projection,
    w_out,
    token_dir,
    tok_logratio,
    segment_ids,
    pair_of_slot,
    pair_counts,
):
    low, wide = jnp.bfloat16, jnp.float32
    section_count = lax.axis_size("section")
    tp_count = lax.axis_size("tp")
    section_index = lax.axis_index("section")
    tp_index = lax.axis_index("tp")
    saved = section_inputs[0]
    batch_groups, rows, width = saved.shape
    token_total = rows * tp_count
    every = batch_groups * token_total
    gain_values = norm_gain[0].astype(wide)
    query_weight = w_query[0]
    key_weight = key_projection[0]
    value_weight = value_projection[0]
    out_weight = w_out[0]
    head_cols = query_weight.shape[1]
    local_heads = head_cols // HEAD_WIDTH
    slice_width, key_width = key_weight.shape
    key_count = key_width // HEAD_WIDTH
    sharers = tp_count // key_count
    seq_count = 2 * SLOTS
    scale = 1.0 / math.sqrt(HEAD_WIDTH)

    ratio_rows = jnp.broadcast_to(tok_logratio.reshape(-1, 1), (batch_groups * rows, 128))
    saved_all, ratio_all, dir_all = exchange(
        (saved, ratio_rows, token_dir), ("all", "all", "last"), 1, 0
    )
    whole = saved_all.transpose(1, 0, 2, 3).reshape(every, width)
    ratios = (
        ratio_all[:, :, 0]
        .reshape(tp_count, batch_groups, rows)
        .transpose(1, 0, 2)
        .reshape(batch_groups, token_total)
    )
    whole_wide = whole.astype(wide)
    whole_inverse = lax.rsqrt(jnp.mean(whole_wide * whole_wide, -1, keepdims=True) + norm_epsilon)
    normed = (whole_wide * whole_inverse * gain_values).astype(low)
    normed_cols = lax.dynamic_slice_in_dim(normed, tp_index * slice_width, slice_width, 1)
    kv_part = jnp.stack(
        [
            jnp.dot(normed_cols, weight, preferred_element_type=wide)
            .astype(low)
            .reshape(every, key_count, HEAD_WIDTH)
            .transpose(1, 0, 2)
            for weight in (key_weight, value_weight)
        ],
        1,
    )
    (kv_all,) = exchange((kv_part,), ("pick",), sharers, 1)
    kv = jnp.sum(kv_all.astype(wide), 0).astype(low)
    keys = kv[0].reshape(batch_groups, token_total, HEAD_WIDTH)
    values = kv[1].reshape(batch_groups, token_total, HEAD_WIDTH)
    queries = jnp.dot(normed, query_weight, preferred_element_type=wide).astype(low)

    member = (
        segment_ids[:, :, None] == jnp.arange(seq_count, dtype=jnp.int32)[None, None, :]
    ).astype(wide)
    seq_sums = jnp.sum(ratios[:, :, None] * member, 1)
    weights = pair_weights(seq_sums, pair_of_slot, pair_counts)
    token_weight = jnp.sum(member * weights[:, None, :], -1)
    top = (
        token_weight.reshape(batch_groups, tp_count, rows)[:, :, :, None]
        * dir_all.transpose(1, 0, 2, 3).astype(wide)
    ).astype(low)

    query_heads = queries.reshape(batch_groups, token_total, local_heads, HEAD_WIDTH)
    position = jnp.arange(token_total, dtype=jnp.int32)
    allowed = (segment_ids[:, :, None] == segment_ids[:, None, :]) & (
        position[:, None] >= position[None, :]
    )[None]
    scores = jnp.einsum("mthc,muc->mhtu", query_heads, keys, preferred_element_type=wide) * scale
    scores = jnp.where(allowed[:, None], scores, masked_score)
    probs = jnp.exp(scores)
    probs = probs / jnp.sum(probs, -1, keepdims=True)
    probs_low = probs.astype(low)
    attended = (
        jnp.einsum("mhtu,muc->mthc", probs_low, values, preferred_element_type=wide)
        .astype(low)
        .reshape(every, head_cols)
    )
    is_last = section_index == section_count - 1
    gain_row = norm_gain[0].reshape(1, width)

    def select(array, pick):
        return lax.dynamic_index_in_dim(array, pick, 0, keepdims=False)

    boundary = jnp.zeros((tp_count, rows, width), low)
    turns = []
    for turn in range(section_count + batch_groups - 1):
        pick = jnp.clip(turn - (section_count - 1 - section_index), 0, batch_groups - 1)
        incoming = jnp.where(is_last, top[min(turn, batch_groups - 1)], boundary)
        upstream = incoming.reshape(token_total, width)
        grad_heads = (
            contract_last(upstream, out_weight)
            .astype(low)
            .reshape(token_total, local_heads, HEAD_WIDTH)
        )
        query_now = select(query_heads, pick)
        key_now = select(keys, pick)
        value_now = select(values, pick)
        probs_now = select(probs, pick)
        probs_low_now = select(probs_low, pick)
        grad_probs = jnp.einsum("thc,uc->htu", grad_heads, value_now, preferred_element_type=wide)
        grad_scores = probs_now * (
            grad_probs - jnp.sum(probs_now * grad_probs, -1, keepdims=True)
        )
        scores_low = (grad_scores * scale).astype(low)
        grad_query = (
            jnp.einsum("htu,uc->thc", scores_low, key_now, preferred_element_type=wide)
            .astype(low)
            .reshape(token_total, head_cols)
        )
        dkv = jnp.stack(
            [
                jnp.einsum("htu,thc->uc", scores_low, query_now, preferred_element_type=wide),
                jnp.einsum("htu,thc->uc", probs_low_now, grad_heads, preferred_element_type=wide),
            ]
        ).astype(low)
        part = contract_last(grad_query, query_weight).astype(low)
        relayed = relay(
            turn,
            batch_groups,
            2 + turn,
            part.reshape(tp_count, rows, width),
            dkv,
            incoming,
            select(saved, pick),
            gain_row,
            key_weight,
            value_weight,
        )
        grad_rows, boundary, dkv_full, gain_part = lax.optimization_barrier(tuple(relayed))
        turns.append((grad_rows, upstream, dkv_full, gain_part, grad_query))

    begin = section_count - 1 - section_index
    grads, upstreams, dkvs, gains, grad_queries = (
        lax.dynamic_slice_in_dim(jnp.stack(values_of), begin, batch_groups, 0)
        for values_of in zip(*turns)
    )
    gain_total = jnp.sum(gains, 0).reshape(8, width // 8)
    (gain_all,) = exchange((gain_total,), ("all",), 1, 2 + len(turns))
    outer = functools.partial(
        lax.dot_general,
        dimension_numbers=(((0,), (0,)), ((), ())),
        preferred_element_type=wide,
    )
    return (
        grads[None],
        outer(normed, grad_queries.reshape(every, head_cols)).astype(low)[None],
        outer(normed_cols, dkvs[:, 0].reshape(every, key_width)).astype(low)[None],
        outer(normed_cols, dkvs[:, 1].reshape(every, key_width)).astype(low)[None],
        outer(attended, upstreams.reshape(every, width)).astype(low)[None],
        jnp.sum(gain_all, 0).reshape(1, width),
    )


def solution(mesh):
    placed = (
        P("section", None, "tp", None),
        P("section", None),
        P("section", None, "tp"),
        P("section", "tp", None),
        P("section", "tp", None),
        P("section", "tp", None),
        P(None, "tp", None),
        P(None, "tp"),
        P(),
        P(),
        P(),
    )
    return jax.shard_map(
        body,
        mesh=mesh,
        in_specs=placed,
        out_specs=(
            P("section", None, "tp", None),
            P("section", None, "tp"),
            P("section", "tp", None),
            P("section", "tp", None),
            P("section", "tp", None),
            P("section", None),
        ),
        check_vma=False,
    )
```

time: 1200 us -> 485 us (0.40)
  waiting for transfers between devices: 771 us -> 0 us
  Pallas kernels: 0 us -> 298 us
  matrix products: 260 us -> 96.6 us
  blocking collectives: 58.5 us -> 0 us
  local copies, waits for them, and re-layouts: 15.9 us -> 59.2 us
  other arithmetic: 54.8 us -> 19.9 us
  starting transfers between devices: 25.3 us -> 0 us
  between operations: 13.9 us -> 1.83 us
    pallas_call x0 -> x8, Pallas kernels: none -> 298 us  [the longest x5 224 us: relay(): pl.pallas_call(functools.partial(relay_kernel, turn, batch_groups, lax.ax...]
    psum x6 -> x0, waiting for transfers between devices: 261 us -> none  [the longest x5 197 us: turn_step(): lax.psum(key_cols.astype(jnp.bfloat16), 'tp').astype(jnp.float32)]
    reduce_scatter x5 -> x0, waiting for transfers between devices: 259 us -> none  [turn_step(): lax.psum_scatter(contract_last(grad_query, query_weight).astype(jnp.bfloa...]
    all_gather x6 -> x0, waiting for transfers between devices: 227 us -> none  [the longest x5 204 us: turn_step(): upstream_full = lax.all_gather(incoming_now, 'tp', axis=0, tiled=True)]
    dot_general x58 -> x29, matrix products: 170 us -> 47.7 us  [the longest x5 9.45 us: body(): jnp.einsum('htu,thc->uc', scores_low, query_now, preferred_element_type=w...]
    psum x2 -> x0, blocking collectives: 58.5 us -> none  [the longest x1 35.1 us: body(): lax.psum(gain_acc.astype(jnp.bfloat16), 'tp').astype(jnp.float32)]
    dot_general x20 -> x10, matrix products: 87.8 us -> 48 us  [contract_last(): lax.dot_general(left, right, (((1,), (1,)), ((), ())), preferred_element_...]
    broadcast_in_dim x5 -> x0, other arithmetic: 22.3 us -> none  [the longest x1 8.98 us: body(): grad_query_w.astype(jnp.bfloat16)[None]]
  transfers between devices with their start and end apart: 27 -> 0, of which waited for: 27 -> 0; matrix products, arithmetic and copies ran while one was open for 18% -> 0% of each run, Pallas kernels for 0% -> 0%
where the time goes in v1:
time: 485 us; the launch traced here: 475 us
  Pallas kernels  298 us (61%)
  matrix products  96.6 us (20%)
  local copies, waits for them, and re-layouts  59.2 us (12%)
  other arithmetic  19.9 us (4%)
    pallas_call x5, Pallas kernels, relay(): pl.pallas_call(functools.partial(relay_kernel, turn, batch_groups, lax.ax...  224 us
    pallas_call x3, Pallas kernels, exchange(): pl.pallas_call(functools.partial(exchange_kernel, kinds, tp_count, group,...  73.8 us
    dot_general x10, matrix products, contract_last(): lax.dot_general(left, right, (((1,), (1,)), ((), ())), preferred_element_...  48 us
    unnamed x119, local copies, waits for them, and re-layouts  23 us

profile of v1, /device:TPU:0, one launch (start us, length us, event | category | flops | bytes accessed | tf_op | source)
XLA Modules:
  0.0 475.3 jit_solution(17763424035127312363)
XLA Ops:
  4.1 1.9 dynamic-slice_bitcast_fusion.1
  7.9 53.5 %exchange_0.1 = (bf16[8,2,8,8192]{3,2,1,0:T(8,128)(2,1)S(1)}, f32[8,16,128]{2,1,0:T(8,128)S(1)}, bf16[8,2,8,8192]{3,2,1,0:T(8,128)(2,1)S(1)}) custom-call(bf16[2,8,8192]{2,1,0:T(8,128)(2,1)S(1)} %bitcast.558, f32[16,128]{1,0:T(8,128)S(1)} %broadcast_in_dim.29.refs_1_, bf16[2,8,8192]{2,1,0:T(8,128)(2,1)S(1)} %copy-done.9), custom_call_target="tpu_custom_call" | custom-call | tf_op jit(solution)/shard_map/exchange_0/pallas_call | solution.py:98
  61.4 1.3 copy-done.3
  65.0 3.4 fusion.29
  69.0 6.5 %fusion.86 = bf16[8,4,8,128]{3,2,1,0:T(8,128)(2,1)S(1)} fusion(bf16[1,512,8192]{2,1,0:T(8,128)(2,1)} %param.16, bf16[2,8,8,8192]{3,2,1,0:T(8,128)(2,1)} %fusion.29, pred[]{:T(512)S(6)} %eq.49), kind=kOutput, calls=%fused_computation.93 | convolution fusion | flops 537427968 | bytes 9502721 | tf_op jit(solution)/shard_map/dot_general | solution.py:33
  76.5 1.3 copy-done.19
  78.5 1.9 fusion.35
  80.4 1.6 reshape.196
  82.0 1.8 constant_dynamic-slice_fusion.4
  86.5 1.7 copy.176
  88.2 1.7 copy.177
  89.8 1.9 convolution_convert_fusion.11
  91.7 1.7 copy.174
  93.4 1.7 copy.175
  96.1 12.6 %exchange_1.1 = bf16[8,2,128,128]{3,2,1,0:T(8,128)(2,1)S(1)} custom-call(bf16[4,2,128,128]{3,2,1,0:T(8,128)(2,1)S(1)} %pad_maximum_fusion.refs_0_), custom_call_target="tpu_custom_call" | custom-call | tf_op jit(solution)/shard_map/exchange_1/pallas_call | solution.py:98
  109.4 1.8 reduce_sum.112
  112.0 1.2 fusion.322
  115.7 1.9 fusion.108
  117.6 1.3 convolution_convert_fusion.16
  120.3 1.5 stack_reshape.28
  121.8 1.1 fusion.38
  123.8 1.6 constant_dynamic-update-slice_fusion.4
  125.4 6.2 %fusion.7.part_ref = bf16[8,8,8192]{2,1,0:T(8,128)(2,1)S(1)} fusion(bf16[1,8192,512]{2,1,0:T(8,128)(2,1)} %param.13, bf16[128,4,64]{0,2,1:T(8,128)(2,1)} %copy-done.28), kind=kOutput, calls=%fused_computation.14 | convolution fusion | flops 537395200 | bytes 9502720 | tf_op jit(solution)/shard_map/dot_general | solution.py:33
  134.2 2.3 copy-done.27
  136.6 2.7 fusion.83
  140.3 1.9 fusion.106
  142.2 1.9 convolution_convert_fusion.15
  144.9 1.5 copy.191
  146.4 1.5 stack_reshape.29
  147.9 1.6 constant_dynamic-update-slice_fusion.3
  149.5 6.2 %fusion.8.part_ref = bf16[8,8,8192]{2,1,0:T(8,128)(2,1)S(1)} fusion(bf16[1,8192,512]{2,1,0:T(8,128)(2,1)} %param.13, bf16[128,4,64]{0,2,1:T(8,128)(2,1)} %convolution_convert_fusion.15), kind=kOutput, calls=%fused_computation.15 | convolution fusion | flops 537395200 | bytes 9502720 | tf_op jit(solution)/shard_map/dot_general | solution.py:33
  157.7 1.3 bitcast_dynamic-update-slice_fusion.2
  159.0 2.7 fusion.80
  162.7 1.9 fusion.104
  164.6 1.9 convolution_convert_fusion.14
  167.3 1.5 copy.196
  168.8 1.5 stack_reshape.30
  170.3 1.6 constant_dynamic-update-slice_fusion.2
  171.9 6.2 %fusion.9.part_ref = bf16[8,8,8192]{2,1,0:T(8,128)(2,1)S(1)} fusion(bf16[1,8192,512]{2,1,0:T(8,128)(2,1)} %param.13, bf16[128,4,64]{0,2,1:T(8,128)(2,1)} %convolution_convert_fusion.14), kind=kOutput, calls=%fused_computation.16 | convolution fusion | flops 537395200 | bytes 9502720 | tf_op jit(solution)/shard_map/dot_general | solution.py:33
  178.1 144.6 %relay_2.1 = (bf16[8,8192]{1,0:T(8,128)(2,1)S(1)}, bf16[8,8,8192]{2,1,0:T(8,128)(2,1)S(1)}, bf16[2,64,512]{2,1,0:T(8,128)(2,1)S(1)}, f32[1,8192]{1,0:T(1,128)S(1)}) custom-call(bf16[8,8,8192]{2,1,0:T(8,128)(2,1)S(1)} %fusion.9.part_ref, bf16[2,64,128]{2,1,0:T(8,128)(2,1)S(1)} %pad_maximum_fusion.3.dkv_ref, bf16[8,8,8192]{2,1,0:T(8,128)(2,1)S(1)} %get-tuple-element.92.g_ref, ...), custom_call_target="tpu_custom_call" | custom-call | tf_op jit(solution)/shard_map/relay_2/pallas_call | solution.py:270
  324.0 1.3 bitcast_dynamic-update-slice_fusion.1
  325.3 2.7 fusion.77
  329.1 1.9 fusion.102
  331.0 1.9 convolution_convert_fusion.13
  333.7 1.5 copy.201
  335.2 1.5 stack_reshape.31
  336.7 1.6 constant_dynamic-update-slice_fusion.1
  338.3 6.2 %fusion.10.part_ref = bf16[8,8,8192]{2,1,0:T(8,128)(2,1)S(1)} fusion(bf16[1,8192,512]{2,1,0:T(8,128)(2,1)} %param.13, bf16[128,4,64]{0,2,1:T(8,128)(2,1)} %convolution_convert_fusion.13), kind=kOutput, calls=%fused_computation.17 | convolution fusion | flops 537395200 | bytes 9502720 | tf_op jit(solution)/shard_map/dot_general | solution.py:33
  344.5 49.8 %relay_3.1 = (bf16[8,8192]{1,0:T(8,128)(2,1)S(1)}, bf16[8,8,8192]{2,1,0:T(8,128)(2,1)S(1)}, bf16[2,64,512]{2,1,0:T(8,128)(2,1)S(1)}, f32[1,8192]{1,0:T(1,128)S(1)}) custom-call(bf16[8,8,8192]{2,1,0:T(8,128)(2,1)S(1)} %fusion.10.part_ref, bf16[2,64,128]{2,1,0:T(8,128)(2,1)S(1)} %pad_maximum_fusion.4.dkv_ref, ...), custom_call_target="tpu_custom_call" | custom-call | tf_op jit(solution)/shard_map/relay_3/pallas_call | solution.py:270
  395.0 1.3 bitcast_dynamic-update-slice_fusion
  396.9 3.1 constant_dynamic-slice_fusion.1
  400.0 2.7 fusion.74
  403.7 1.8 fusion.100
  405.5 1.3 convolution_convert_fusion.12
  408.3 1.5 stack_reshape.32
  409.8 1.5 constant_dynamic-update-slice_fusion
  411.2 1.6 constant_dynamic-slice_fusion.3
  412.8 6.1 %fusion.11.part_ref = bf16[8,8,8192]{2,1,0:T(8,128)(2,1)S(1)} fusion(bf16[1,8192,512]{2,1,0:T(8,128)(2,1)} %param.13, bf16[128,4,64]{0,2,1:T(8,128)(2,1)S(1)} %convolution_convert_fusion.12), kind=kOutput, calls=%fused_computation.18 | convolution fusion | flops 537395200 | bytes 9502720 | tf_op jit(solution)/shard_map/dot_general | solution.py:33
  418.9 28.3 %relay_4.1 = (bf16[8,8192]{1,0:T(8,128)(2,1)S(1)}, bf16[8,8,8192]{2,1,0:T(8,128)(2,1)}, bf16[2,64,512]{2,1,0:T(8,128)(2,1)S(1)}, f32[1,8192]{1,0:T(1,128)S(1)}) custom-call(bf16[8,8,8192]{2,1,0:T(8,128)(2,1)S(1)} %fusion.11.part_ref, bf16[2,64,128]{2,1,0:T(8,128)(2,1)S(1)} %pad_maximum_fusion.5.dkv_ref, bf16[8,8,8192]{2,1,0:T(8,128)(2,1)S(1)} %get-tuple-element.110.g_ref, ...), custom_call_target="tpu_custom_call" | custom-call | tf_op jit(solution)/shard_map/relay_4/pallas_call | solution.py:270
  448.4 7.7 %exchange_7.1 = f32[8,8,1024]{2,1,0:T(8,128)S(1)} custom-call(f32[8,1024]{1,0:T(8,128)S(1)} %reshape.219.refs_0_), custom_call_target="tpu_custom_call" | custom-call | tf_op jit(solution)/shard_map/exchange_7/pallas_call | solution.py:98
  456.9 2.4 fusion.30
  459.2 2.4 fusion.31
  461.6 7.5 %fusion.5 = bf16[1,8192,512]{2,1,0:T(8,128)(2,1)} fusion(bf16[128,8192]{1,0:T(8,128)(2,1)} %bitcast.575, bf16[128,512]{1,0:T(8,128)(2,1)S(1)} %bitcast.589), kind=kOutput, calls=%fused_computation.7 | convolution fusion | flops 1077936128 | bytes 10616832 | tf_op jit(solution)/shard_map/dot_general | solution.py:456
  469.1 5.8 %fusion.6 = bf16[1,512,8192]{2,1,0:T(8,128)(2,1)} fusion(bf16[128,8192]{1,0:T(8,128)(2,1)S(1)} %bitcast.576, bf16[16,8,4,128]{3,2,1,0:T(4,128)(2,1)S(1)} %bitcast.596), kind=kOutput, calls=%fused_computation.8 | convolution fusion | flops 1077936128 | bytes 10616832 | tf_op jit(solution)/shard_map/dot_general | solution.py:459
  (183 shorter events, 36.5 us)
Async XLA Ops:
  6.0 0.9 copy-start.2
  7.0 0.9 copy-start.9
  61.4 1.3 copy-start.3
  69.0 6.6 %copy-start.14 = (bf16[2,8,8,8192]{3,2,1,0:T(8,128)(2,1)S(1)}, bf16[2,8,8,8192]{3,2,1,0:T(8,128)(2,1)}, u32[]{:S(2)}) copy-start(bf16[2,8,8,8192]{3,2,1,0:T(8,128)(2,1)} %fusion.29) | copy-start | bytes 6291460
  69.0 8.8 %slice-start = ((s8[8388608]{0:T(1024)(128)(4,1)}), s8[4194304]{0:T(1024)(128)(4,1)S(1)}, s32[]{:S(2)}) async-start(s8[8388608]{0:T(1024)(128)(4,1)} %bitcast.564), calls=%async_computation | async-start | bytes 8388608
  75.6 2.9 slice-start.1
  76.5 1.3 copy-start.19
  84.3 1.2 copy-start
  84.3 5.5 %copy-start.1 = (bf16[1,1024,512]{2,1,0:T(8,128)(2,1)S(1)}, bf16[1,1024,512]{2,1,0:T(8,128)(2,1)}, u32[]{:S(2)}) copy-start(bf16[1,1024,512]{2,1,0:T(8,128)(2,1)} %param.14) | copy-start | bytes 3145732
  84.8 0.7 copy-start.21
  108.6 0.8 copy-start.4
  112.0 6.9 %copy-start.35 = (bf16[1,128,128]{2,1,0:T(8,128)(2,1)}, bf16[1,128,128]{2,1,0:T(8,128)(2,1)S(1)}, u32[]{:S(2)}) copy-start(bf16[1,128,128]{2,1,0:T(8,128)(2,1)S(1)} %get-tuple-element.153) | copy-start | bytes 98308
  112.0 27.5 %copy-start.29 = (bf16[1,128,128]{2,1,0:T(8,128)(2,1)}, bf16[1,128,128]{2,1,0:T(8,128)(2,1)S(1)}, u32[]{:S(2)}) copy-start(bf16[1,128,128]{2,1,0:T(8,128)(2,1)S(1)} %get-tuple-element.154) | copy-start | bytes 98308
  114.0 0.7 copy-start.22
  118.9 4.8 %copy-start.28 = (bf16[128,4,64]{0,2,1:T(8,128)(2,1)}, bf16[128,4,64]{0,2,1:T(8,128)(2,1)S(1)}, u32[]{:S(2)}) copy-start(bf16[128,4,64]{0,2,1:T(8,128)(2,1)S(1)} %convolution_convert_fusion.16) | copy-start | bytes 196612
  123.7 12.8 %slice-start.2 = ((s8[8388608]{0:T(1024)(128)(4,1)}), s8[4194304]{0:T(1024)(128)(4,1)S(1)}, s32[]{:S(2)}) async-start(s8[8388608]{0:T(1024)(128)(4,1)} %bitcast.566), calls=%async_computation.2 | async-start | bytes 8388608
  125.4 6.2 %copy-start.5 = (bf16[1,8192]{1,0:T(2,128)(2,1)S(1)}, bf16[1,8192]{1,0:T(2,128)(2,1)}, u32[]{:S(2)}) copy-start(bf16[1,8192]{1,0:T(2,128)(2,1)} %gain_ref.4) | copy-start | bytes 49156
  125.4 6.2 %copy-start.8 = (bf16[8,8192]{1,0:T(8,128)(2,1)S(1)}, bf16[8,8192]{1,0:T(8,128)(2,1)}, u32[]{:S(2)}) copy-start(bf16[8,8192]{1,0:T(8,128)(2,1)} %get-tuple-element.75.saved_ref) | copy-start | bytes 393220
  125.4 11.2 %slice-start.3 = ((s8[8388608]{0:T(1024)(128)(4,1)}), s8[4194304]{0:T(1024)(128)(4,1)S(1)}, s32[]{:S(2)}) async-start(s8[8388608]{0:T(1024)(128)(4,1)} %bitcast.566), calls=%async_computation.3 | async-start | bytes 8388608
  131.6 2.2 copy-start.15
  134.2 2.4 copy-start.27
  136.5 2.7 copy-start.23
  136.5 5.7 %copy-start.36 = (bf16[1,128,128]{2,1,0:T(8,128)(2,1)S(1)}, bf16[1,128,128]{2,1,0:T(8,128)(2,1)}, u32[]{:S(2)}) copy-start(bf16[1,128,128]{2,1,0:T(8,128)(2,1)} %copy-done.35) | copy-start | bytes 98308
  147.9 11.1 %slice-start.4 = ((s8[8388608]{0:T(1024)(128)(4,1)}), s8[4194304]{0:T(1024)(128)(4,1)S(1)}, s32[]{:S(2)}) async-start(s8[8388608]{0:T(1024)(128)(4,1)} %bitcast.568), calls=%async_computation.4 | async-start | bytes 8388608
  149.5 6.2 %copy-start.7 = (bf16[8,8192]{1,0:T(8,128)(2,1)S(1)}, bf16[8,8192]{1,0:T(8,128)(2,1)}, u32[]{:S(2)}) copy-start(bf16[8,8192]{1,0:T(8,128)(2,1)} %get-tuple-element.84.saved_ref) | copy-start | bytes 393220
  149.5 9.5 %slice-start.5 = ((s8[8388608]{0:T(1024)(128)(4,1)}), s8[4194304]{0:T(1024)(128)(4,1)S(1)}, s32[]{:S(2)}) async-start(s8[8388608]{0:T(1024)(128)(4,1)} %bitcast.568), calls=%async_computation.5 | async-start | bytes 8388608
  155.7 2.0 copy-start.16
  159.0 2.7 copy-start.24
  159.0 2.9 copy-start.30
  159.0 5.7 %copy-start.37 = (bf16[1,128,128]{2,1,0:T(8,128)(2,1)S(1)}, bf16[1,128,128]{2,1,0:T(8,128)(2,1)}, u32[]{:S(2)}) copy-start(bf16[1,128,128]{2,1,0:T(8,128)(2,1)} %copy-done.35) | copy-start | bytes 98308
  170.3 155.0 %slice-start.6 = ((s8[8388608]{0:T(1024)(128)(4,1)}), s8[4194304]{0:T(1024)(128)(4,1)S(1)}, s32[]{:S(2)}) async-start(s8[8388608]{0:T(1024)(128)(4,1)} %bitcast.570), calls=%async_computation.6 | async-start | bytes 8388608
  171.9 6.2 %copy-start.6 = (bf16[8,8192]{1,0:T(8,128)(2,1)S(1)}, bf16[8,8192]{1,0:T(8,128)(2,1)}, u32[]{:S(2)}) copy-start(bf16[8,8192]{1,0:T(8,128)(2,1)} %get-tuple-element.93.saved_ref) | copy-start | bytes 393220
  171.9 153.4 %slice-start.7 = ((s8[8388608]{0:T(1024)(128)(4,1)}), s8[4194304]{0:T(1024)(128)(4,1)S(1)}, s32[]{:S(2)}) async-start(s8[8388608]{0:T(1024)(128)(4,1)} %bitcast.570), calls=%async_computation.7 | async-start | bytes 8388608
  178.1 145.9 %copy-start.17 = (bf16[2,8,8,8192]{3,2,1,0:T(8,128)(2,1)S(1)}, bf16[2,8,8,8192]{3,2,1,0:T(8,128)(2,1)}, u32[]{:S(2)}) copy-start(bf16[2,8,8,8192]{3,2,1,0:T(8,128)(2,1)} %fusion.29) | copy-start | bytes 6291460
  322.7 5.3 %copy-start.10 = (f32[1,8192]{1,0:T(1,128)}, f32[1,8192]{1,0:T(1,128)S(1)}, u32[]{:S(2)}) copy-start(f32[1,8192]{1,0:T(1,128)S(1)} %get-tuple-element.126) | copy-start | bytes 98308
  325.3 2.7 copy-start.25
  325.3 2.9 copy-start.31
  325.3 5.7 %copy-start.38 = (bf16[1,128,128]{2,1,0:T(8,128)(2,1)S(1)}, bf16[1,128,128]{2,1,0:T(8,128)(2,1)}, u32[]{:S(2)}) copy-start(bf16[1,128,128]{2,1,0:T(8,128)(2,1)} %copy-done.35) | copy-start | bytes 98308
  336.7 63.3 %slice-start.8 = ((s8[8388608]{0:T(1024)(128)(4,1)}), s8[4194304]{0:T(1024)(128)(4,1)S(1)}, s32[]{:S(2)}) async-start(s8[8388608]{0:T(1024)(128)(4,1)} %bitcast.572), calls=%async_computation.8 | async-start | bytes 8388608
  338.3 61.7 %slice-start.9 = ((s8[8388608]{0:T(1024)(128)(4,1)}), s8[4194304]{0:T(1024)(128)(4,1)S(1)}, s32[]{:S(2)}) async-start(s8[8388608]{0:T(1024)(128)(4,1)} %bitcast.572), calls=%async_computation.9 | async-start | bytes 8388608
  344.5 50.5 %copy-start.18 = (bf16[2,8,8,8192]{3,2,1,0:T(8,128)(2,1)S(1)}, bf16[2,8,8,8192]{3,2,1,0:T(8,128)(2,1)}, u32[]{:S(2)}) copy-start(bf16[2,8,8,8192]{3,2,1,0:T(8,128)(2,1)} %fusion.29) | copy-start | bytes 6291460
  394.3 8.4 %copy-start.12 = (f32[1,8192]{1,0:T(1,128)}, f32[1,8192]{1,0:T(1,128)S(1)}, u32[]{:S(2)}) copy-start(f32[1,8192]{1,0:T(1,128)S(1)} %get-tuple-element.127) | copy-start | bytes 98308
  400.0 2.7 copy-start.26
  400.0 2.9 copy-start.32
  400.0 5.6 %copy-start.39 = (bf16[1,128,128]{2,1,0:T(8,128)(2,1)S(1)}, bf16[1,128,128]{2,1,0:T(8,128)(2,1)}, u32[]{:S(2)}) copy-start(bf16[1,128,128]{2,1,0:T(8,128)(2,1)} %copy-done.35) | copy-start | bytes 98308
  403.1 0.7 copy-start.42
  412.8 34.4 %copy-start.40 = (bf16[5,8,8192]{2,1,0:T(8,128)(2,1)S(1)}, bf16[5,8,8192]{2,1,0:T(8,128)(2,1)}, u32[]{:S(2)}) copy-start(bf16[5,8,8192]{2,1,0:T(8,128)(2,1)} %bitcast_dynamic-update-slice_fusion.11) | copy-start | bytes 1966084
  412.8 35.2 %copy-start.41 = (bf16[5,2,64,512]{3,2,1,0:T(8,128)(2,1)S(1)}, bf16[5,2,64,512]{3,2,1,0:T(8,128)(2,1)}, u32[]{:S(2)}) copy-start(bf16[5,2,64,512]{3,2,1,0:T(8,128)(2,1)} %bitcast_dynamic-update-slice_fusion.6) | copy-start | bytes 1966084
  418.9 29.1 %copy-start.11 = (f32[1,8192]{1,0:T(1,128)S(1)}, f32[1,8192]{1,0:T(1,128)}, u32[]{:S(2)}) copy-start(f32[1,8192]{1,0:T(1,128)} %copy-done.10) | copy-start | bytes 98308
  418.9 29.1 %copy-start.13 = (f32[1,8192]{1,0:T(1,128)S(1)}, f32[1,8192]{1,0:T(1,128)}, u32[]{:S(2)}) copy-start(f32[1,8192]{1,0:T(1,128)} %copy-done.12) | copy-start | bytes 98308
  447.2 14.4 %copy-start.33 = (bf16[2,64,512]{2,1,0:T(8,128)(2,1)S(1)}, bf16[2,64,512]{2,1,0:T(8,128)(2,1)}, u32[]{:S(2)}) copy-start(bf16[2,64,512]{2,1,0:T(8,128)(2,1)} %constant_dynamic-slice_fusion.3) | copy-start | bytes 393220
  461.6 7.5 %copy-start.20 = (bf16[2,64,8192]{2,1,0:T(8,128)(2,1)S(1)}, bf16[2,64,8192]{2,1,0:T(8,128)(2,1)}, u32[]{:S(2)}) copy-start(bf16[2,64,8192]{2,1,0:T(8,128)(2,1)} %constant_dynamic-slice_fusion.1) | copy-start | bytes 6291460
  461.6 7.5 %copy-start.34 = (bf16[2,64,4,128]{3,2,1,0:T(4,128)(2,1)S(1)}, bf16[2,64,4,128]{3,2,1,0:T(4,128)(2,1)}, u32[]{:S(2)}) copy-start(bf16[2,64,4,128]{3,2,1,0:T(4,128)(2,1)} %copy.215) | copy-start | bytes 393220
